TPU v7x, 512 devices: a whole 4x8x8 slice. The times are simulated.
512 devices in a mesh: batch: 4 (over x_hi, core), space: 128 (over x_lo, y, z).
Axes of the slice: x: 4 (x_hi: 2, x_lo: 2; x = x_hi * 2 + x_lo), y: 8, z: 8, core: 2. Of those that a mesh axis runs over, the one named last changes fastest.
Arguments:
- inputs: bfloat16 [4, 32, 128, 128, 128], P('batch', None, None, 'space'), may hold values from -6 to 6
- pre_act: bfloat16 [4, 32, 128, 128, 128], P('batch', None, None, 'space'), may hold values from -8 to 8
- cotangent: bfloat16 [4, 32, 128, 128, 128], P('batch', None, None, 'space'), may hold values from -6 to 6
- spectral_weight: bfloat16 [2, 32, 32, 16384], P(None, None, None, 'space'), may hold values from -6 to 6
- skip_weight: bfloat16 [32, 32], replicated, may hold values from -1 to 1
Outputs:
- grad_inputs: bfloat16 [4, 32, 128, 128, 128], P('batch', None, None, 'space')
- grad_spectral: float32 [2, 32, 32, 16384], P(None, None, 'batch', 'space')
- grad_skip: float32 [32, 32], replicated
All inputs are finite; a program needn't handle non-finite values.
Results may differ from a plain program's by a relative error of at most 0.0055.
Values sent between devices are 32-bit elements; how exact they have to be, the bound alone decides.
A program may use at most 64 MiB of HBM per device.

v0:
```python
import math
import jax
import jax.numpy as jnp
from jax import lax
from jax.sharding import PartitionSpec as P

NX = 128
NY = 128
NZ = 128
MX = 16
MY = 16
MZ = 16
HIGHEST = lax.Precision.HIGHEST


def phase_table(length, count, signed):
    points = jnp.arange(length, dtype=jnp.int32)
    orders = jnp.arange(count, dtype=jnp.int32)
    if signed:
        orders = jnp.where(orders < count // 2, orders, orders - count)
    residues = jnp.mod(points[:, None] * orders[None, :], length)
    radians = residues.astype(jnp.float32) * (2.0 * math.pi / length)
    return (jnp.cos(radians), jnp.sin(radians))


def forward_block(cosine, sine):
    return jnp.stack(
        [jnp.stack([cosine, -sine], axis=1), jnp.stack([sine, cosine], axis=1)], axis=0
    )


def inverse_block(cosine, sine):
    cos_rows = cosine.T
    sin_rows = sine.T
    return jnp.stack(
        [jnp.stack([cos_rows, sin_rows], axis=1), jnp.stack([-sin_rows, cos_rows], axis=1)], axis=0
    )


def gelu_slope(values):
    normal_cdf = 0.5 * (1.0 + jax.scipy.special.erf(values * (1.0 / math.sqrt(2.0))))
    density = jnp.exp(-0.5 * values * values) * (1.0 / math.sqrt(2.0 * math.pi))
    return normal_cdf + values * density


def local_spectrum(grid_in):
    cos_x, sin_x = phase_table(NX, 2 * MX, True)
    table_x = jnp.stack([cos_x, -sin_x], axis=1).astype(jnp.bfloat16)
    section_x = jnp.einsum(
        "scxyz,xpa->scpayz", grid_in, table_x, preferred_element_type=jnp.float32
    )
    cos_z, sin_z = phase_table(NZ, MZ, False)
    section_z = jnp.einsum(
        "scpayz,pzqk->scqyak", section_x, forward_block(cos_z, sin_z), precision=HIGHEST
    )
    return section_z.reshape(
        section_z.shape[0], section_z.shape[1], 2, section_z.shape[3], 2 * MX * MZ
    )


def along_y(spectra):
    cos_y, sin_y = phase_table(NY, 2 * MY, True)
    section_y = jnp.einsum(
        "scpym,pyqk->scqmk", spectra, forward_block(cos_y, sin_y), precision=HIGHEST
    )
    return section_y.reshape(section_y.shape[0], section_y.shape[1], 2, section_y.shape[3] * 2 * MY)


def both_along_y(spectra_pair):
    return (along_y(spectra_pair[0]), along_y(spectra_pair[1]))


def to_grid(spectra):
    shaped = spectra.reshape(spectra.shape[0], spectra.shape[1], 2, spectra.shape[3], 2 * MX, MZ)
    cos_z, sin_z = phase_table(NZ, MZ, False)
    grid_z = jnp.einsum(
        "scpyak,pkqz->scqayz", shaped, inverse_block(cos_z, sin_z), precision=HIGHEST
    )
    cos_x, sin_x = phase_table(NX, 2 * MX, True)
    table_x = jnp.stack([cos_x.T, -sin_x.T], axis=0)
    return jnp.einsum("scpayz,pax->scxyz", grid_z, table_x, precision=HIGHEST)


def cross_terms(spec_left, spec_right):
    real_part = jnp.einsum(
        "sim,som->iom", spec_left[:, :, 0], spec_right[:, :, 0], precision=HIGHEST
    )
    real_part = real_part + jnp.einsum(
        "sim,som->iom", spec_left[:, :, 1], spec_right[:, :, 1], precision=HIGHEST
    )
    imag_part = jnp.einsum(
        "sim,som->iom", spec_left[:, :, 0], spec_right[:, :, 1], precision=HIGHEST
    )
    imag_part = imag_part - jnp.einsum(
        "sim,som->iom", spec_left[:, :, 1], spec_right[:, :, 0], precision=HIGHEST
    )
    return jnp.stack([real_part, imag_part], axis=0)


def contract(weight_part, spec_part):
    return jnp.einsum("iom,som->sim", weight_part, spec_part, preferred_element_type=jnp.float32)


def skip_gradient(grid_in, cot_pre):
    partial_sum = jnp.einsum(
        "sixyz,soxyz->io", grid_in, cot_pre, preferred_element_type=jnp.float32
    )
    summed = lax.psum(partial_sum, ("batch", "space"))
    return summed / math.sqrt(grid_in.shape[0] * lax.axis_size("batch") * NX * NY * NZ)


def on_device(inputs, pre_act, cotangent, spectral_weight, skip_weight):
    samples = inputs.shape[0]
    channels = inputs.shape[1]
    slope_pre = gelu_slope(pre_act.astype(jnp.float32))
    cot_pre = (cotangent.astype(jnp.float32) * slope_pre).astype(jnp.bfloat16)
    spec_u, spec_e = both_along_y(
        (
            lax.all_to_all(
                local_spectrum(inputs), "space", split_axis=4, concat_axis=3, tiled=True
            ),
            lax.all_to_all(
                local_spectrum(cot_pre), "space", split_axis=4, concat_axis=3, tiled=True
            ),
        )
    )
    mode_count = spec_u.shape[3]
    position = jnp.arange(mode_count, dtype=jnp.int32)
    kxz_index = lax.axis_index("space") * (mode_count // (2 * MY)) + position // (2 * MY)
    mode_weights = jnp.where(kxz_index % MZ == 0, 1.0, 2.0).astype(jnp.float32) / float(
        NX * NY * NZ
    )
    mode_grad = lax.psum_scatter(
        cross_terms(spec_u, spec_e), "batch", scatter_dimension=2, tiled=True
    )
    grad_spectral = mode_grad * mode_weights
    rounded = spec_e.astype(jnp.bfloat16)
    weight_real = spectral_weight[0]
    weight_imag = spectral_weight[1]
    back_real = contract(weight_real, rounded[:, :, 0]) + contract(weight_imag, rounded[:, :, 1])
    back_imag = contract(weight_real, rounded[:, :, 1]) - contract(weight_imag, rounded[:, :, 0])
    back_modes = jnp.stack([back_real, back_imag], axis=2) * mode_weights
    shaped = back_modes.reshape(samples, channels, 2, mode_count // (2 * MY), 2 * MY)
    cos_y, sin_y = phase_table(NY, 2 * MY, True)
    grid_y = jnp.einsum("scpmk,pkqy->scqym", shaped, inverse_block(cos_y, sin_y), precision=HIGHEST)
    spatial = to_grid(lax.all_to_all(grid_y, "space", split_axis=3, concat_axis=4, tiled=True))
    mixed = jnp.einsum("io,soxyz->sixyz", skip_weight, cot_pre, preferred_element_type=jnp.float32)
    grad_inputs = (spatial + mixed).astype(jnp.bfloat16)
    grad_skip = skip_gradient(inputs, cot_pre)
    return (grad_inputs, grad_spectral, grad_skip)


def solution(mesh):
    placed = (
        P("batch", None, None, "space", None),
        P("batch", None, None, "space", None),
        P("batch", None, None, "space", None),
        P(None, None, None, "space"),
        P(),
    )
    return jax.shard_map(
        on_device,
        mesh=mesh,
        in_specs=placed,
        out_specs=(P("batch", None, None, "space", None), P(None, None, "batch", "space"), P()),
        check_vma=False,
    )
```

profile of v0, /device:TPU:2, one launch (start us, length us, event | category | flops | bytes accessed | tf_op | source)
XLA Modules:
  0.0 209.4 jit_solution(695585654018447)
XLA Ops:
  7.3 0.2 fusion.73
  7.5 2.3 %fusion.8 = bf16[1,32,128,1,128]{4,2,3,1,0:T(8,128)(2,1)S(1)} fusion(bf16[1,32,128,1,128]{4,2,3,1,0:T(8,128)(2,1)} %param.6, bf16[1,32,128,1,128]{4,2,3,1,0:T(8,128)(2,1)} %param.7), kind=kLoop, calls=%fused_computation.13 | loop fusion | flops 6291456 | bytes 3145728 | tf_op jit(solution)/shard_map/convert_element_type | solution.py:116
  9.8 0.3 convolution_bitcast_fusion.2
  10.1 2.5 %convolution_bitcast_fusion.4 = f32[1,32,2,1,32,16]{4,5,1,2,3,0:T(8,128)S(1)} fusion(f32[32,2,32,128]{3,2,0,1:T(8,128)S(1)} %convolution_bitcast_fusion.2, f32[1,128,2,16]{1,3,0,2:T(8,128)S(1)} %get-tuple-element.33, f32[1,128,2,16]{1,3,0,2:T(8,128)S(1)} %get-tuple-element.32), kind=kOutput, calls=%fused_computation.19 | convolution fusion | flops 100671488 | bytes 1212416 | tf_op jit(solution)/shard_map/scpayz,pzqk->scqyak/dot_general | solution.py:53
  12.6 0.4 copy.55
  12.9 0.4 copy.162
  13.3 1.2 reshape.693
  14.5 18.7 %all-to-all-start = ((f32[128,1,256]{2,1,0:T(1,128)}), f32[128,1,256]{2,1,0:T(1,128)S(1)}, u32[]{:S(2)}, u32[]{:S(2)}) async-start(f32[128,1,256]{2,1,0:T(1,128)} %reshape.693), calls=%async_computation | async-start | bytes 262144 | tf_op jit(solution)/shard_map/all_to_all | solution.py:122
  33.4 0.2 fusion.75
  33.6 0.3 convolution_bitcast_fusion.1
  33.9 2.5 %convolution_bitcast_fusion.3 = f32[1,32,2,1,32,16]{4,5,1,2,3,0:T(8,128)S(1)} fusion(f32[32,2,32,128]{3,2,0,1:T(8,128)S(1)} %convolution_bitcast_fusion.1, f32[1,128,2,16]{1,3,0,2:T(8,128)S(1)} %get-tuple-element.33, f32[1,128,2,16]{1,3,0,2:T(8,128)S(1)} %get-tuple-element.32), kind=kOutput, calls=%fused_computation.18 | convolution fusion | flops 100671488 | bytes 1212416 | tf_op jit(solution)/shard_map/scpayz,pzqk->scqyak/dot_general | solution.py:53
  36.4 1.3 convolution_bitcast_fusion.6
  37.7 2.1 fusion.18
  39.8 0.4 copy.69
  40.1 0.4 copy.161
  40.5 1.2 reshape.697
  41.7 96.8 %psum.7 = f32[32,32]{0,1:T(8,128)S(1)} all-reduce(f32[32,32]{0,1:T(8,128)S(1)} %convolution_bitcast_fusion.6), channel_id=1, replica_groups=mesh['batch'=4,'space'=128] {'batch','space'}, use_global_device_ids=true, to_apply=%region_1.2 | all-reduce | flops 1024 | bytes 8192 | tf_op jit(solution)/shard_map/psum | solution.py:108
  138.6 11.8 %all-to-all-start.2 = ((f32[128,1,256]{2,1,0:T(1,128)}), f32[128,1,256]{2,1,0:T(1,128)S(1)}, u32[]{:S(2)}, u32[]{:S(2)}) async-start(f32[128,1,256]{2,1,0:T(1,128)} %reshape.697), calls=%async_computation.2 | async-start | bytes 262144 | tf_op jit(solution)/shard_map/all_to_all | solution.py:119
  150.4 0.5 broadcast.824
  150.9 0.9 reduce.8
  151.9 0.4 reshape.694
  152.3 0.3 copy.59
  152.6 0.5 fusion.28
  153.2 9.8 %all-to-all-done.2 = f32[128,1,256]{2,1,0:T(1,128)S(1)} async-done(((f32[128,1,256]{2,1,0:T(1,128)}), f32[128,1,256]{2,1,0:T(1,128)S(1)}, u32[]{:S(2)}, u32[]{:S(2)}) %all-to-all-start.2) | async-done | bytes 131104 | tf_op jit(solution)/shard_map/all_to_all | solution.py:119
  163.0 0.9 reduce.10
  163.9 0.4 reshape.698
  164.4 0.3 copy.73
  164.7 0.5 fusion.25
  165.2 0.1 copy.76
  165.3 0.2 add_bitcast_fusion
  165.5 1.1 pad_maximum_fusion
  166.8 0.4 fusion.22
  167.2 0.1 stack.145
  167.3 0.1 stack.144
  167.5 0.3 convolution_bitcast_fusion.5
  167.8 0.3 copy.61
  168.1 1.0 reshape.695
  169.1 7.0 %all-to-all-start.1 = ((f32[128,1,256]{2,1,0:T(1,128)}), f32[128,1,256]{2,1,0:T(1,128)S(1)}, u32[]{:S(2)}, u32[]{:S(2)}) async-start(f32[128,1,256]{2,1,0:T(1,128)} %reshape.695), calls=%async_computation.1 | async-start | bytes 262144 | tf_op jit(solution)/shard_map/all_to_all | solution.py:146
  176.2 0.7 copy.80
  176.8 0.2 fusion.79
  177.0 11.7 %all-to-all-done.1 = f32[128,1,256]{2,1,0:T(1,128)S(1)} async-done(((f32[128,1,256]{2,1,0:T(1,128)}), f32[128,1,256]{2,1,0:T(1,128)S(1)}, u32[]{:S(2)}, u32[]{:S(2)}) %all-to-all-start.1) | async-done | bytes 131104 | tf_op jit(solution)/shard_map/all_to_all | solution.py:146
  188.7 0.9 reduce.9
  189.7 1.0 reshape.696
  190.7 1.9 copy.62
  192.6 2.3 %copy.63 = f32[32,2,32,16]{2,3,1,0:T(8,128)} copy(f32[32,2,32,16]{0,3,2,1:T(8,128)} %bitcast.256) | data formatting | bytes 262144 | tf_op jit(solution)/shard_map/reshape.31
  194.9 2.1 convolution_bitcast_fusion
  197.0 3.9 %fusion.9 = bf16[1,32,128,1,128]{4,2,3,1,0:T(8,128)(2,1)} fusion(f32[128,128,32]{1,2,0:T(8,128)S(1)} %copy-done.1, f32[32,2,32,128]{3,2,0,1:T(8,128)S(1)} %convolution_bitcast_fusion, f32[1,32,128]{2,1,0:T(8,128)S(1)} %get-tuple-element.35, f32[1,32,128]{2,1,0:T(8,128)S(1)} %get-tuple-element.34), kind=kOutput, calls=%fused_computation.15 | convolution fusion | flops 403709952 | bytes 4227072 | tf_op jit(solution)/shard_map/scpayz,pax->scxyz/dot_general | solution.py:81
  200.9 1.7 broadcast_multiply_fusion
  (36 shorter events, 0.8 us)
Async XLA Ops:
  7.2 26.4 %copy-start = (bf16[1,32,128,1,128]{4,2,3,1,0:T(8,128)(2,1)S(1)}, bf16[1,32,128,1,128]{4,2,3,1,0:T(8,128)(2,1)}, u32[]{:S(2)}) copy-start(bf16[1,32,128,1,128]{4,2,3,1,0:T(8,128)(2,1)} %param.5) | copy-start | bytes 3145732
  14.5 124.0 %all-to-all-start = ((f32[128,1,256]{2,1,0:T(1,128)}), f32[128,1,256]{2,1,0:T(1,128)S(1)}, u32[]{:S(2)}, u32[]{:S(2)}) async-start(f32[128,1,256]{2,1,0:T(1,128)} %reshape.693), calls=%async_computation | async-start | bytes 262144 | tf_op jit(solution)/shard_map/all_to_all | solution.py:122
  33.9 3.8 %copy-start.3 = (bf16[32,32]{1,0:T(8,128)(2,1)S(1)}, bf16[32,32]{1,0:T(8,128)(2,1)}, u32[]{:S(2)}) copy-start(bf16[32,32]{1,0:T(8,128)(2,1)} %param.9) | copy-start | bytes 6148
  138.6 24.4 %all-to-all-start.2 = ((f32[128,1,256]{2,1,0:T(1,128)}), f32[128,1,256]{2,1,0:T(1,128)S(1)}, u32[]{:S(2)}, u32[]{:S(2)}) async-start(f32[128,1,256]{2,1,0:T(1,128)} %reshape.697), calls=%async_computation.2 | async-start | bytes 262144 | tf_op jit(solution)/shard_map/all_to_all | solution.py:119
  150.4 50.5 %reduce-scatter.2.cloned.1.call-start = ((), (), s32[]{:S(2)}) async-start(), calls=%async_computation.4 | async-start | bytes 1310720 | tf_op jit(solution)/shard_map/reduce_scatter | solution.py:133
  165.5 1.3 copy-start.2
  169.1 19.6 %all-to-all-start.1 = ((f32[128,1,256]{2,1,0:T(1,128)}), f32[128,1,256]{2,1,0:T(1,128)S(1)}, u32[]{:S(2)}, u32[]{:S(2)}) async-start(f32[128,1,256]{2,1,0:T(1,128)} %reshape.695), calls=%async_computation.1 | async-start | bytes 262144 | tf_op jit(solution)/shard_map/all_to_all | solution.py:146
  189.7 7.3 %copy-start.1 = (f32[128,128,32]{1,2,0:T(8,128)S(1)}, f32[128,128,32]{1,2,0:T(8,128)}, u32[]{:S(2)}) copy-start(f32[128,128,32]{1,2,0:T(8,128)} %fusion.18) | copy-start | bytes 6291460
Sparse Core Ops, SparseCore 0:
  166.7 31.4 reduce-scatter.1
where the time goes:
time: 210 us; the launch traced here: 209 us
  blocking collectives  96.8 us (46%)
  starting transfers between devices  37.6 us (18%)
  waiting for transfers between devices  21.5 us (10%)
  matrix products  16.1 us (8%)
  between operations  14.4 us (7%)
  local copies, waits for them, and re-layouts  13.7 us (7%)
  other arithmetic  9.26 us (4%)
    psum x1, blocking collectives, skip_gradient(): summed = lax.psum(partial_sum, ('batch', 'space'))  96.8 us
    all_to_all x1, starting transfers between devices, on_device(): lax.all_to_all(local_spectrum(cot_pre), 'space', split_axis=4, concat_axi...  18.7 us
    all_to_all x1, starting transfers between devices, on_device(): lax.all_to_all(local_spectrum(inputs), 'space', split_axis=4, concat_axis...  11.8 us
    all_to_all x1, waiting for transfers between devices, on_device(): lax.all_to_all(grid_y, 'space', split_axis=3, concat_axis=4, tiled=True)  11.7 us
    all_to_all x1, waiting for transfers between devices, on_device(): lax.all_to_all(local_spectrum(inputs), 'space', split_axis=4, concat_axis...  9.75 us
    all_to_all x1, starting transfers between devices, on_device(): lax.all_to_all(grid_y, 'space', split_axis=3, concat_axis=4, tiled=True)  7.05 us
    unnamed x17, local copies, waits for them, and re-layouts  6.13 us
    dot_general x2, matrix products, local_spectrum(): jnp.einsum('scpayz,pzqk->scqyak', section_x, forward_block(cos_z, sin_z),...  4.95 us
  transfers between devices with their start and end apart: 4, of which 2 were waited for; matrix products, arithmetic and copies ran while one was open for 13% of the time, Pallas kernels for 0%

commit v1 on v0

--- a/solution.py
+++ b/solution.py
@@ -105,7 +105,7 @@
     partial_sum = jnp.einsum(
         "sixyz,soxyz->io", grid_in, cot_pre, preferred_element_type=jnp.float32
     )
-    summed = lax.psum(partial_sum, ("batch", "space"))
+    summed = lax.psum(lax.psum(partial_sum, "space"), "batch")
     return summed / math.sqrt(grid_in.shape[0] * lax.axis_size("batch") * NX * NY * NZ)
 
 

time: 210 us -> 732 us (3.49)
  the two profiles are of different devices: /device:TPU:2 before, /device:TPU:1 now
where the time goes in v1:
time: 732 us; the launch traced here: 731 us
  blocking collectives  623 us (85%)
  starting transfers between devices  31.9 us (4%)
  waiting for transfers between devices  23.1 us (3%)
  matrix products  16.1 us (2%)
  between operations  14.4 us (2%)
  local copies, waits for them, and re-layouts  13.7 us (2%)
  other arithmetic  9.02 us (1%)
    psum x2, blocking collectives, skip_gradient(): summed = lax.psum(lax.psum(partial_sum, 'space'), 'batch')  623 us
    all_to_all x1, starting transfers between devices, on_device(): lax.all_to_all(local_spectrum(cot_pre), 'space', split_axis=4, concat_axi...  19.3 us
  transfers between devices with their start and end apart: 4, of which 3 were waited for; matrix products, arithmetic and copies ran while one was open for 4% of the time, Pallas kernels for 0%

profile of v1, /device:TPU:1, one launch (start us, length us, event | category | flops | bytes accessed | tf_op | source)
XLA Modules:
  0.0 731.4 jit_solution(7930233129228965550)
XLA Ops:
  7.3 0.2 fusion.73
  7.5 2.3 fusion.8
  9.8 0.3 convolution_bitcast_fusion.2
  10.1 2.5 convolution_bitcast_fusion.4
  12.6 0.4 copy.55
  12.9 0.4 copy.162
  13.3 1.2 reshape.693
  14.5 19.3 %all-to-all-start = ((f32[128,1,256]{2,1,0:T(1,128)}), f32[128,1,256]{2,1,0:T(1,128)S(1)}, u32[]{:S(2)}, u32[]{:S(2)}) async-start(f32[128,1,256]{2,1,0:T(1,128)} %reshape.693), calls=%async_computation | async-start | bytes 262144 | tf_op jit(solution)/shard_map/all_to_all | solution.py:122
  34.0 0.2 fusion.75
  34.1 0.3 convolution_bitcast_fusion.1
  34.5 2.5 convolution_bitcast_fusion.3
  36.9 1.3 convolution_bitcast_fusion.6
  38.2 2.1 fusion.18
  40.3 0.4 copy.69
  40.7 0.4 copy.161
  41.1 1.2 reshape.697
  42.3 499.8 %psum.14 = f32[32,32]{0,1:T(8,128)S(1)} all-reduce(f32[32,32]{0,1:T(8,128)S(1)} %convolution_bitcast_fusion.6), channel_id=1, replica_groups=mesh['batch'=4,'space'=128] {'space'}, use_global_device_ids=true, to_apply=%region_1.2 | all-reduce | flops 1024 | bytes 8192 | tf_op jit(solution)/shard_map/psum | solution.py:108
  542.1 123.3 %psum.15 = f32[32,32]{0,1:T(8,128)S(1)} all-reduce(f32[32,32]{0,1:T(8,128)S(1)} %psum.14), channel_id=1, replica_groups=mesh['batch'=4,'space'=128] {'batch'}, use_global_device_ids=true, to_apply=%region_2.3 | all-reduce | flops 1024 | bytes 8192 | tf_op jit(solution)/shard_map/psum | solution.py:108
  665.5 6.2 all-to-all-start.2
  671.7 0.5 broadcast.824
  672.2 0.8 reduce.8
  673.0 0.4 reshape.694
  673.5 0.3 copy.59
  673.8 0.5 fusion.28
  674.4 9.6 %all-to-all-done.2 = f32[128,1,256]{2,1,0:T(1,128)S(1)} async-done(((f32[128,1,256]{2,1,0:T(1,128)}), f32[128,1,256]{2,1,0:T(1,128)S(1)}, u32[]{:S(2)}, u32[]{:S(2)}) %all-to-all-start.2) | async-done | bytes 131104 | tf_op jit(solution)/shard_map/all_to_all | solution.py:119
  684.0 0.8 reduce.10
  684.8 0.4 reshape.698
  685.3 0.3 copy.73
  685.6 0.5 fusion.25
  686.2 0.2 add_bitcast_fusion
  686.4 1.1 pad_maximum_fusion
  687.7 0.4 fusion.22
  688.1 0.1 stack.145
  688.4 0.3 convolution_bitcast_fusion.5
  688.7 0.3 copy.61
  689.0 1.0 reshape.695
  690.0 6.4 all-to-all-start.1
  696.4 0.7 copy.80
  697.1 0.2 fusion.79
  697.2 11.2 %all-to-all-done.1 = f32[128,1,256]{2,1,0:T(1,128)S(1)} async-done(((f32[128,1,256]{2,1,0:T(1,128)}), f32[128,1,256]{2,1,0:T(1,128)S(1)}, u32[]{:S(2)}, u32[]{:S(2)}) %all-to-all-start.1) | async-done | bytes 131104 | tf_op jit(solution)/shard_map/all_to_all | solution.py:146
  708.5 0.8 reduce.9
  709.3 1.0 reshape.696
  710.4 1.9 copy.62
  712.3 2.3 copy.63
  714.6 2.1 convolution_bitcast_fusion
  716.7 3.9 fusion.9
  720.6 2.3 reduce-scatter.2.cloned.1.call-done
  722.9 1.7 broadcast_multiply_fusion
  (37 shorter events, 1.0 us)
Async XLA Ops:
  7.2 27.0 %copy-start = (bf16[1,32,128,1,128]{4,2,3,1,0:T(8,128)(2,1)S(1)}, bf16[1,32,128,1,128]{4,2,3,1,0:T(8,128)(2,1)}, u32[]{:S(2)}) copy-start(bf16[1,32,128,1,128]{4,2,3,1,0:T(8,128)(2,1)} %param.5) | copy-start | bytes 3145732
  14.5 650.9 %all-to-all-start = ((f32[128,1,256]{2,1,0:T(1,128)}), f32[128,1,256]{2,1,0:T(1,128)S(1)}, u32[]{:S(2)}, u32[]{:S(2)}) async-start(f32[128,1,256]{2,1,0:T(1,128)} %reshape.693), calls=%async_computation | async-start | bytes 262144 | tf_op jit(solution)/shard_map/all_to_all | solution.py:122
  34.4 3.8 copy-start.3
  665.5 18.5 %all-to-all-start.2 = ((f32[128,1,256]{2,1,0:T(1,128)}), f32[128,1,256]{2,1,0:T(1,128)S(1)}, u32[]{:S(2)}, u32[]{:S(2)}) async-start(f32[128,1,256]{2,1,0:T(1,128)} %reshape.697), calls=%async_computation.2 | async-start | bytes 262144 | tf_op jit(solution)/shard_map/all_to_all | solution.py:119
  671.7 51.2 %reduce-scatter.2.cloned.1.call-start = ((), (), s32[]{:S(2)}) async-start(), calls=%async_computation.4 | async-start | bytes 1310720 | tf_op jit(solution)/shard_map/reduce_scatter | solution.py:133
  686.4 1.3 copy-start.2
  690.0 18.5 %all-to-all-start.1 = ((f32[128,1,256]{2,1,0:T(1,128)}), f32[128,1,256]{2,1,0:T(1,128)S(1)}, u32[]{:S(2)}, u32[]{:S(2)}) async-start(f32[128,1,256]{2,1,0:T(1,128)} %reshape.695), calls=%async_computation.1 | async-start | bytes 262144 | tf_op jit(solution)/shard_map/all_to_all | solution.py:146
  709.3 7.4 %copy-start.1 = (f32[128,128,32]{1,2,0:T(8,128)S(1)}, f32[128,128,32]{1,2,0:T(8,128)}, u32[]{:S(2)}) copy-start(f32[128,128,32]{1,2,0:T(8,128)} %fusion.18) | copy-start | bytes 6291460
Sparse Core Ops, SparseCore 0:
  687.6 35.2 reduce-scatter.1
